TPU v7x, 32 devices: a whole 2x2x4 slice. The times are simulated.
32 devices in a mesh: dp: 8 (over z, y), tensor: 4 (over x, core).
Axes of the slice: x: 2, y: 2, z: 4, core: 2. Of those that a mesh axis runs over, the one named last changes fastest.
Arguments:
- tokens: bfloat16 [8192, 1024], P(('dp', 'tensor')), may hold values from -6 to 6
- cotangent: float32 [8192, 1024], P(('dp', 'tensor')), may hold values from -6 to 6
- lengths: int32 [8, 2], P('dp'), may hold values from 64 to 512, as said below
- order: int32 [8, 1024], P('dp'), may hold values from 0 to 1023, each once within a row
- adapter_ids: int32 [8, 2], P('dp'), may hold values from 0 to 7
- norm1_gain: float32 [1024], replicated, may hold values from 0.25 to 1.75
- norm1_shift: float32 [1024], replicated, may hold values from -1.5 to 1.5
- qkv_weight: bfloat16 [1024, 3, 1024], P(None, None, 'tensor'), may hold values from -0.1875 to 0.1875
- qv_bias: float32 [2, 1024], P(None, 'tensor'), may hold values from -1.5 to 1.5
- proj_weight: bfloat16 [1024, 1024], P('tensor'), may hold values from -1.5 to 1.5
- proj_bias: float32 [1024], replicated, may hold values from -1.5 to 1.5
- norm2_gain: float32 [1024], replicated, may hold values from 0.25 to 1.75
- norm2_shift: float32 [1024], replicated, may hold values from -1.5 to 1.5
- up_weight: bfloat16 [1024, 4096], P(None, 'tensor'), may hold values from -0.1875 to 0.1875
- up_bias: float32 [4096], P('tensor'), may hold values from -1.5 to 1.5
- down_weight: bfloat16 [4096, 1024], P('tensor'), may hold values from -0.09375 to 0.09375
- down_bias: float32 [1024], replicated, may hold values from -1.5 to 1.5
- adapt_qkv_in: bfloat16 [1024, 128], replicated, may hold values from -0.1875 to 0.1875
- adapt_qkv_out: bfloat16 [128, 3, 1024], P(None, None, 'tensor'), may hold values from -0.75 to 0.75
- adapt_proj_in: bfloat16 [1024, 128], P('tensor'), may hold values from -0.75 to 0.75
- adapt_proj_out: bfloat16 [128, 1024], replicated, may hold values from -0.75 to 0.75
- adapt_up_in: bfloat16 [1024, 128], replicated, may hold values from -0.1875 to 0.1875
- adapt_up_out: bfloat16 [128, 4096], P(None, 'tensor'), may hold values from -0.75 to 0.75
- adapt_down_in: bfloat16 [4096, 128], P('tensor'), may hold values from -0.09375 to 0.09375
- adapt_down_out: bfloat16 [128, 1024], replicated, may hold values from -0.75 to 0.75
Outputs:
- result: float32 [8192, 1024], P(('dp', 'tensor'))
- grad_input: float32 [8192, 1024], P(('dp', 'tensor'))
- grad_qkv_in: float32 [1024, 128], replicated
- grad_qkv_out: float32 [128, 3, 1024], P(None, None, 'tensor')
- grad_proj_in: float32 [1024, 128], P('tensor')
- grad_proj_out: float32 [128, 1024], replicated
- grad_up_in: float32 [1024, 128], replicated
- grad_up_out: float32 [128, 4096], P(None, 'tensor')
- grad_down_in: float32 [4096, 128], P('tensor')
- grad_down_out: float32 [128, 1024], replicated
Inputs may be any that keep to these rules, and one draw needn't show every extreme that they name: `lengths`: in every group one sequence has exactly 512 valid tokens; the others have at least 512 // 8 (and at least one). `order`: each row is a permutation of the group's 1024 stored rows.
All inputs are finite; a program needn't handle non-finite values.
Results may differ from a plain program's by a relative error of at most 0.023.
Values may be sent and summed in bfloat16 or wider, within the bound.
No kernel may reach another device: no remote copies, remote signals or barrier semaphores. Data moves between devices by JAX's collectives and lax.ppermute only.
A program may use at most 128 MiB of HBM per device.

v0:
```python
import math
import jax
import jax.numpy as jnp
from jax import lax
from jax.sharding import PartitionSpec as P

D = 1024
HD = 64
RANK = 16
EPSILON = 1e-05
NEGATIVE = -1000000000.0


def layer_norm(values, gain, shift):
    centre = values - jnp.mean(values, -1, keepdims=True)
    spread = jnp.mean(centre * centre, -1, keepdims=True)
    return centre * lax.rsqrt(spread + EPSILON) * gain + shift


def matmul(left, right):
    return jnp.dot(left, right, preferred_element_type=jnp.float32)


def matmul_back(left, right):
    return lax.dot_general(
        left, right, (((1,), (1,)), ((), ())), preferred_element_type=jnp.float32
    )


def matmul_over(left, right):
    return lax.dot_general(
        left, right, (((0,), (0,)), ((), ())), preferred_element_type=jnp.float32
    )


def gelu_tanh(values):
    return jax.nn.gelu(values, approximate=True)


def block_scores(queries, keys, query_start, length):
    scale = 1.0 / math.sqrt(HD)
    scores = jnp.einsum("qhc,khc->hqk", queries, keys, preferred_element_type=jnp.float32) * scale
    query_pos = query_start + jnp.arange(queries.shape[0], dtype=jnp.int32)
    key_pos = jnp.arange(keys.shape[0], dtype=jnp.int32)
    allowed = (key_pos[None, :] <= query_pos[:, None]) & (key_pos[None, :] < length)
    return jnp.where(allowed[None], scores, NEGATIVE)


def attention_forward(qkv_seq, lengths_row, seq_len):
    group_rows = qkv_seq.shape[0]
    heads_here = qkv_seq.shape[2] // HD
    block_rows = min(512, seq_len)
    per_seq = seq_len // block_rows
    split = qkv_seq.reshape(group_rows, 3, heads_here, HD)

    def one_block(block_id):
        seq_id = block_id // per_seq
        query_start = block_id % per_seq * block_rows
        base = seq_id * seq_len
        queries = lax.dynamic_slice_in_dim(split[:, 0], base + query_start, block_rows, 0)
        keys = lax.dynamic_slice_in_dim(split[:, 1], base, seq_len, 0)
        values = lax.dynamic_slice_in_dim(split[:, 2], base, seq_len, 0)
        scores = block_scores(queries, keys, query_start, lengths_row[seq_id])
        top = jnp.max(scores, -1, keepdims=True)
        weights = jnp.exp(scores - top)
        total = jnp.sum(weights, -1, keepdims=True)
        probs = (weights / total).astype(jnp.bfloat16)
        attended = jnp.einsum("hqk,khc->qhc", probs, values, preferred_element_type=jnp.float32)
        return (attended.reshape(block_rows, heads_here * HD), (top + jnp.log(total))[..., 0])

    blocks = group_rows // block_rows
    outputs, log_totals = lax.map(one_block, jnp.arange(blocks, dtype=jnp.int32))
    return (outputs.reshape(group_rows, heads_here * HD), log_totals)


def attention_backward(qkv_seq, grad_seq, log_totals, lengths_row, seq_len):
    group_rows = qkv_seq.shape[0]
    heads_here = qkv_seq.shape[2] // HD
    block_rows = min(512, seq_len)
    per_seq = seq_len // block_rows
    seqs = group_rows // seq_len
    scale = 1.0 / math.sqrt(HD)
    split = qkv_seq.reshape(group_rows, 3, heads_here, HD)
    grad_split = grad_seq.reshape(group_rows, heads_here, HD)

    def one_block(block_id):
        seq_id = block_id // per_seq
        query_start = block_id % per_seq * block_rows
        base = seq_id * seq_len
        queries = lax.dynamic_slice_in_dim(split[:, 0], base + query_start, block_rows, 0)
        keys = lax.dynamic_slice_in_dim(split[:, 1], base, seq_len, 0)
        values = lax.dynamic_slice_in_dim(split[:, 2], base, seq_len, 0)
        grad_block = lax.dynamic_slice_in_dim(grad_split, base + query_start, block_rows, 0)
        scores = block_scores(queries, keys, query_start, lengths_row[seq_id])
        probs = jnp.exp(scores - log_totals[block_id][..., None])
        grad_probs = jnp.einsum(
            "qhc,khc->hqk", grad_block, values, preferred_element_type=jnp.float32
        )
        centre = jnp.sum(probs * grad_probs, -1, keepdims=True)
        grad_raw = (probs * (grad_probs - centre) * scale).astype(jnp.bfloat16)
        grad_query = jnp.einsum("hqk,khc->qhc", grad_raw, keys, preferred_element_type=jnp.float32)
        grad_key = jnp.einsum("hqk,qhc->khc", grad_raw, queries, preferred_element_type=jnp.float32)
        grad_value = jnp.einsum(
            "hqk,qhc->khc",
            probs.astype(jnp.bfloat16),
            grad_block,
            preferred_element_type=jnp.float32,
        )
        return (grad_query, grad_key, grad_value)

    blocks = group_rows // block_rows
    grad_query, grad_key, grad_value = lax.map(one_block, jnp.arange(blocks, dtype=jnp.int32))
    width_here = heads_here * HD
    grad_query = grad_query.reshape(group_rows, width_here)
    grad_key = jnp.sum(grad_key.reshape(seqs, per_seq, seq_len, width_here), axis=1).reshape(
        group_rows, width_here
    )
    grad_value = jnp.sum(grad_value.reshape(seqs, per_seq, seq_len, width_here), axis=1).reshape(
        group_rows, width_here
    )
    return jnp.stack([grad_query, grad_key, grad_value], 1)


def body(
    tokens,
    cotangent,
    lengths,
    order,
    adapter_ids,
    norm1_gain,
    norm1_shift,
    qkv_weight,
    qv_bias,
    proj_weight,
    proj_bias,
    norm2_gain,
    norm2_shift,
    up_weight,
    up_bias,
    down_weight,
    down_bias,
    adapt_qkv_in,
    adapt_qkv_out,
    adapt_proj_in,
    adapt_proj_out,
    adapt_up_in,
    adapt_up_out,
    adapt_down_in,
    adapt_down_out,
):
    own_rows = tokens.shape[0]
    order_row = order[0]
    lengths_row = lengths[0]
    ids_row = adapter_ids[0]
    group_rows = order_row.shape[0]
    seqs = lengths_row.shape[0]
    seq_len = group_rows // seqs
    adapt_cols = adapt_qkv_in.shape[1]
    rank_index = lax.axis_index("tensor")
    inverse = (
        jnp.zeros((group_rows,), jnp.int32)
        .at[order_row]
        .set(jnp.arange(group_rows, dtype=jnp.int32))
    )
    seq_of = inverse // seq_len
    adapter_of = jnp.sum(
        jnp.where(
            seq_of[:, None] == jnp.arange(seqs, dtype=jnp.int32)[None, :], ids_row[None, :], 0
        ),
        axis=1,
    )
    group_mask = (
        jnp.arange(adapt_cols, dtype=jnp.int32)[None, :] // RANK == adapter_of[:, None]
    ).astype(jnp.float32)
    own_mask = lax.dynamic_slice_in_dim(group_mask, rank_index * own_rows, own_rows, 0)
    bias_three = jnp.stack([qv_bias[0], jnp.zeros_like(qv_bias[0]), qv_bias[1]])
    proj_joined = jnp.concatenate([proj_weight, adapt_proj_in], 1)
    down_joined = jnp.concatenate([down_weight, adapt_down_in], 1)
    up_joined = jnp.concatenate([up_weight, adapt_up_out], 0)
    qkv_joined = jnp.concatenate([qkv_weight, adapt_qkv_out], 0)

    def project_qkv(rows_all, lowrank_all):
        value = jnp.einsum("rd,dkc->rkc", rows_all, qkv_weight, preferred_element_type=jnp.float32)
        value = value + jnp.einsum(
            "ra,akc->rkc", lowrank_all, adapt_qkv_out, preferred_element_type=jnp.float32
        )
        return (value + bias_three[None]).astype(jnp.bfloat16)

    def project_up(rows_all, lowrank_all):
        return matmul(rows_all, up_weight) + matmul(lowrank_all, adapt_up_out) + up_bias

    inputs = tokens.astype(jnp.float32)
    normed1 = layer_norm(inputs, norm1_gain, norm1_shift).astype(jnp.bfloat16)
    low1 = (matmul(normed1, adapt_qkv_in) * own_mask).astype(jnp.bfloat16)
    normed1_all, low1_small = (
        lax.all_gather(normed1, "tensor", axis=0, tiled=True),
        lax.all_gather(low1, "tensor", axis=0, tiled=True),
    )
    low1_all = low1_small
    qkv_arr = project_qkv(normed1_all, low1_all)
    qkv_seq = jnp.take(qkv_arr, order_row, axis=0)
    attended_seq, log_totals = attention_forward(qkv_seq, lengths_row, seq_len)
    attended = jnp.take(attended_seq.astype(jnp.bfloat16), inverse, axis=0)
    rows = attended
    mask_rows = group_mask
    part = matmul(rows, proj_joined)
    summed_attn = lax.psum_scatter(
        jnp.concatenate([part[:, :D], part[:, D:] * mask_rows], 1).astype(jnp.bfloat16),
        "tensor",
        scatter_dimension=0,
        tiled=True,
    ).astype(jnp.float32)
    proj_low = summed_attn[:, D:].astype(jnp.bfloat16)
    mid = inputs + summed_attn[:, :D] + matmul(proj_low, adapt_proj_out) + proj_bias
    normed2 = layer_norm(mid, norm2_gain, norm2_shift).astype(jnp.bfloat16)
    low2 = (matmul(normed2, adapt_up_in) * own_mask).astype(jnp.bfloat16)
    normed2_all, low2_small = (
        lax.all_gather(normed2, "tensor", axis=0, tiled=True),
        lax.all_gather(low2, "tensor", axis=0, tiled=True),
    )
    low2_all = low2_small
    upper = project_up(normed2_all, low2_all)
    active = gelu_tanh(upper).astype(jnp.bfloat16)
    rows = active
    mask_rows = group_mask
    part = matmul(rows, down_joined)
    summed_mlp = lax.psum_scatter(
        jnp.concatenate([part[:, :D], part[:, D:] * mask_rows], 1).astype(jnp.bfloat16),
        "tensor",
        scatter_dimension=0,
        tiled=True,
    ).astype(jnp.float32)
    down_low = summed_mlp[:, D:].astype(jnp.bfloat16)
    result = mid + summed_mlp[:, :D] + matmul(down_low, adapt_down_out) + down_bias
    grad_mlp = cotangent.astype(jnp.bfloat16)
    grad_down_low = (matmul_back(grad_mlp, adapt_down_out) * own_mask).astype(jnp.bfloat16)
    grad_down_out_part = matmul_over(down_low, grad_mlp)
    grad_mlp_all, grad_down_small = (
        lax.all_gather(grad_mlp, "tensor", axis=0, tiled=True),
        lax.all_gather(grad_down_low, "tensor", axis=0, tiled=True),
    )
    normed2_again, low2_again_small = (
        lax.all_gather(normed2, "tensor", axis=0, tiled=True),
        lax.all_gather(low2, "tensor", axis=0, tiled=True),
    )
    upper = project_up(normed2_again, low2_again_small)
    active = gelu_tanh(upper).astype(jnp.bfloat16)
    low2_all = low2_again_small
    grad_active = matmul_back(grad_mlp_all, down_weight) + matmul_back(
        grad_down_small, adapt_down_in
    )
    grad_down_in_part = matmul_over(active, grad_down_small)
    gelu_value, gelu_pull = jax.vjp(gelu_tanh, upper)
    grad_upper = gelu_pull(grad_active)[0].astype(jnp.bfloat16)
    grad_up_out_part = matmul_over(low2_all, grad_upper)
    rows = grad_upper
    part = matmul_back(rows, up_joined)
    summed_up = lax.psum_scatter(
        jnp.concatenate([part[:, :D], part[:, D:]], 1).astype(jnp.bfloat16),
        "tensor",
        scatter_dimension=0,
        tiled=True,
    ).astype(jnp.float32)
    grad_low2 = (summed_up[:, D:] * own_mask).astype(jnp.bfloat16)
    grad_up_in_part = matmul_over(normed2, grad_low2)
    grad_normed2 = summed_up[:, :D] + matmul_back(grad_low2, adapt_up_in)
    norm2_value, norm2_pull = jax.vjp(
        lambda values: layer_norm(values, norm2_gain, norm2_shift), mid
    )
    grad_mid = cotangent + norm2_pull(grad_normed2)[0]
    grad_attn = grad_mid.astype(jnp.bfloat16)
    grad_proj_low = (matmul_back(grad_attn, adapt_proj_out) * own_mask).astype(jnp.bfloat16)
    grad_proj_out_part = matmul_over(proj_low, grad_attn)
    grad_attn_all, grad_proj_small = (
        lax.all_gather(grad_attn, "tensor", axis=0, tiled=True),
        lax.all_gather(grad_proj_low, "tensor", axis=0, tiled=True),
    )
    grad_attended = matmul_back(grad_attn_all, proj_weight) + matmul_back(
        grad_proj_small, adapt_proj_in
    )
    grad_proj_in_part = matmul_over(attended, grad_proj_small)
    grad_attended_seq = jnp.take(grad_attended, order_row, axis=0).astype(jnp.bfloat16)
    normed1_again, low1_again_small = (
        lax.all_gather(normed1, "tensor", axis=0, tiled=True),
        lax.all_gather(low1, "tensor", axis=0, tiled=True),
    )
    qkv_seq = jnp.take(project_qkv(normed1_again, low1_again_small), order_row, axis=0)
    low1_all = low1_again_small
    grad_qkv_seq = attention_backward(qkv_seq, grad_attended_seq, log_totals, lengths_row, seq_len)
    grad_qkv = jnp.take(grad_qkv_seq.astype(jnp.bfloat16), inverse, axis=0)
    grad_qkv_out_part = jnp.einsum(
        "ra,rkc->akc", low1_all, grad_qkv, preferred_element_type=jnp.float32
    )
    rows = grad_qkv
    part = jnp.einsum("rkc,dkc->rd", rows, qkv_joined, preferred_element_type=jnp.float32)
    summed_qkv = lax.psum_scatter(
        jnp.concatenate([part[:, :D], part[:, D:]], 1).astype(jnp.bfloat16),
        "tensor",
        scatter_dimension=0,
        tiled=True,
    ).astype(jnp.float32)
    grad_low1 = (summed_qkv[:, D:] * own_mask).astype(jnp.bfloat16)
    grad_qkv_in_part = matmul_over(normed1, grad_low1)
    grad_normed1 = summed_qkv[:, :D] + matmul_back(grad_low1, adapt_qkv_in)
    norm1_value, norm1_pull = jax.vjp(
        lambda values: layer_norm(values, norm1_gain, norm1_shift), inputs
    )
    grad_input = grad_mid + norm1_pull(grad_normed1)[0]
    wide = lax.psum(
        (grad_qkv_in_part, grad_proj_out_part, grad_up_in_part, grad_down_out_part),
        ("dp", "tensor"),
    )
    narrow = (
        lax.psum(grad_qkv_out_part.astype(jnp.bfloat16), "dp").astype(jnp.float32),
        lax.psum(grad_proj_in_part.astype(jnp.bfloat16), "dp").astype(jnp.float32),
        lax.psum(grad_up_out_part.astype(jnp.bfloat16), "dp").astype(jnp.float32),
        lax.psum(grad_down_in_part.astype(jnp.bfloat16), "dp").astype(jnp.float32),
    )
    return (
        result,
        grad_input,
        wide[0],
        narrow[0],
        narrow[1],
        wide[1],
        wide[2],
        narrow[2],
        narrow[3],
        wide[3],
    )


def solution(mesh):
    in_specs = (
        P(("dp", "tensor"), None),
        P(("dp", "tensor"), None),
        P("dp", None),
        P("dp", None),
        P("dp", None),
        P(),
        P(),
        P(None, None, "tensor"),
        P(None, "tensor"),
        P("tensor", None),
        P(),
        P(),
        P(),
        P(None, "tensor"),
        P("tensor"),
        P("tensor", None),
        P(),
        P(),
        P(None, None, "tensor"),
        P("tensor", None),
        P(),
        P(),
        P(None, "tensor"),
        P("tensor", None),
        P(),
    )
    out_specs = (
        P(("dp", "tensor"), None),
        P(("dp", "tensor"), None),
        P(),
        P(None, None, "tensor"),
        P("tensor", None),
        P(),
        P(),
        P(None, "tensor"),
        P("tensor", None),
        P(),
    )
    return jax.shard_map(body, mesh=mesh, in_specs=in_specs, out_specs=out_specs, check_vma=False)
```

profile of v0, /device:TPU:0, one launch (start us, length us, event | category | flops | bytes accessed | tf_op | source)
XLA Modules:
  0.0 638.7 jit_solution(10005724395536461428)
XLA Ops:
  9.8 2.1 fusion.106
  12.8 4.3 scatter_custom_fusion
  20.2 8.9 %all_gather.29 = bf16[1024,128]{1,0:T(8,128)(2,1)S(1)} all-gather(bf16[256,128]{1,0:T(8,128)(2,1)S(1)} %fusion.97), channel_id=1, replica_groups=mesh['dp'=8,'tensor'=4] {'tensor'}, dimensions={0}, use_global_device_ids=true | all-gather | bytes 327680 | tf_op jit(solution)/shard_map/all_gather | solution.py:197
  31.9 6.9 %all-gather.5.cloned.1.call-done = bf16[1024,1024]{1,0:T(8,128)(2,1)} async-done(((bf16[256,1024]{1,0:T(8,128)(2,1)}), bf16[1024,1024]{1,0:T(8,128)(2,1)}) %all-gather.5.cloned.1.call-update) | async-done | bytes 2097168 | tf_op jit(solution)/shard_map/all_gather | solution.py:196
  38.8 3.8 fusion.84
  43.3 2.7 copy.65
  46.0 10.1 %gather_fusion.2 = bf16[1024,3,256]{2,1,0:T(4,128)(2,1)} fusion(bf16[1024,3,256]{2,1,0:T(4,128)(2,1)} %copy.65, s32[1024]{0:T(1024)S(1)} %fusion.129), kind=kCustom, calls=%fused_computation.clone | custom fusion | bytes 3149824 | tf_op jit(solution)/shard_map/jit(_take)/gather | solution.py:201
  56.1 6.3 broadcast_select_fusion.1
  62.4 2.9 copy.66
  65.3 15.9 %while.32 = (s32[]{:T(128)}, bf16[2,512,256]{1,2,0:T(8,128)(2,1)S(1)}, f32[2,4,512]{2,1,0:T(4,128)S(1)}, bf16[1024,3,4,64]{0,3,2,1:T(8,128)(2,1)S(1)}, s32[2]{0:...) while((s32[]{:T(128)}, ...), condition=%wide.region_7.9_spmd, body=%wide.region_4.8_spmd.sunk | while | flops 281541120 | bytes 18417900 | solution.py:72
  81.4 4.4 gather_fusion
  85.9 1.8 fusion.108
  91.6 32.2 %reduce-scatter.5.cloned.1.call-done = bf16[256,1152]{1,0:T(8,128)(2,1)} async-done(((bf16[1024,1152]{1,0:T(8,128)(2,1)}), bf16[256,1152]{1,0:T(8,128)(2,1)}) %reduce-scatter.5.cloned.1.call-update) | async-done | bytes 589840 | tf_op jit(solution)/shard_map/reduce_scatter | solution.py:207
  125.7 1.7 add_convert_fusion.1
  129.0 6.4 %all_gather.33 = bf16[1024,128]{1,0:T(8,128)(2,1)} all-gather(bf16[256,128]{1,0:T(8,128)(2,1)S(1)} %fusion.99), channel_id=1, replica_groups=mesh['dp'=8,'tensor'=4] {'tensor'}, dimensions={0}, use_global_device_ids=true | all-gather | bytes 327680 | tf_op jit(solution)/shard_map/all_gather | solution.py:240
  135.4 13.3 %all-gather.9.cloned.1.call-done = bf16[1024,1024]{1,0:T(8,128)(2,1)} async-done(((bf16[256,1024]{1,0:T(8,128)(2,1)}), bf16[1024,1024]{1,0:T(8,128)(2,1)}) %all-gather.9.cloned.1.call-update) | async-done | bytes 2097168 | tf_op jit(solution)/shard_map/all_gather | solution.py:239
  148.7 6.6 %fusion.153 = f32[1024,1024]{1,0:T(8,128)} fusion(bf16[1024,1024]{1,0:T(8,128)(2,1)} %all-gather.9.cloned.1.call-done, bf16[1024,1024]{1,0:T(8,128)(2,1)} %param.46), kind=kOutput, calls=%fused_computation.219 | convolution fusion | flops 2147483648 | bytes 8388608 | tf_op jit(solution)/shard_map/dot_general | solution.py:25
  155.6 5.8 all_gather.31
  161.4 12.0 %all-gather.7.cloned.1.call-done = bf16[1024,1024]{1,0:T(8,128)(2,1)} async-done(((bf16[256,1024]{1,0:T(8,128)(2,1)}), bf16[1024,1024]{1,0:T(8,128)(2,1)}) %all-gather.7.cloned.1.call-update) | async-done | bytes 2097168 | tf_op jit(solution)/shard_map/all_gather | solution.py:218
  173.4 4.6 fusion.152
  178.7 2.1 copy-done.18
  181.8 3.2 fusion.76
  186.5 4.2 convolution_convert_fusion
  190.7 33.2 %reduce-scatter.9.cloned.1.call-done = bf16[256,1152]{1,0:T(8,128)(2,1)} async-done(((bf16[1024,1152]{1,0:T(8,128)(2,1)}), bf16[256,1152]{1,0:T(8,128)(2,1)}) %reduce-scatter.9.cloned.1.call-update) | async-done | bytes 589840 | tf_op jit(solution)/shard_map/reduce_scatter | solution.py:258
  229.6 6.5 %fusion.77 = bf16[1024,1152]{1,0:T(8,128)(2,1)S(1)} fusion(bf16[1024,128]{1,0:T(8,128)(2,1)S(1)} %copy-done.64, bf16[1024,1024]{1,0:T(8,128)(2,1)} %param.46, f32[1024,1024]{1,0:T(8,128)} %copy-done.18), kind=kOutput, calls=%fused_computation.87 | convolution fusion | flops 2430074880 | bytes 8912896 | tf_op jit(solution)/shard_map/dot_general | solution.py:21
  240.9 4.8 convolution_convert_fusion.1
  246.1 6.3 all_gather.35
  252.3 2.2 convolution_convert_fusion.4
  254.6 2.4 fusion.154
  257.4 5.5 gather_fusion.1
  262.9 2.1 copy.68
  266.1 62.1 %while.33 = (s32[]{:T(128)}, bf16[2,512,4,64]{1,3,2,0:T(8,128)(2,1)}, bf16[2,512,4,64]{1,3,2,0:T(8,128)(2,1)}, bf16[2,512,4,64]{1,3,2,0:T(8,128)(2,1)}, bf16[102...) while((s32[]{:T(128)}, ...), condition=%wide.region_17.19_spmd, body=%wide.region_15.18_spmd.sunk | while | flops 686298624 | bytes 57437636 | solution.py:112
  271.6 2.8 fusion.230
  274.4 3.3 subtract_exponential_fusion.3
  277.6 7.9 %fusion.232 = bf16[2,512,4,64]{1,3,2,0:T(8,128)(2,1)} fusion(bf16[2,512,4,64]{1,3,2,0:T(8,128)(2,1)} %get-tuple-element.493, s32[]{:T(128)S(6)} %copy.112, f32[4,512,512]{1,2,0:T(8,128)} %subtract_exponential_fusion.3, f32[4,512,512]{1,2,0:T(8,128)} %fusion.230, bf16[1024,1,4,64]{0,3,2,1:T(8,128)(2,1)} %copy-done.5, s32[]{:T(128)S(6)} %select_n.203), kind=kOutput, calls=%fused_computation.43.clone.1 | convolution fusion | flops 139463168 | bytes 17563656 | tf_op jit(solution)/shard_map/while/body/eval_jaxpr/hqk,qhc->khc/dot_general | solution.py:102
  285.6 8.0 %fusion.231 = bf16[2,512,4,64]{1,3,2,0:T(8,128)(2,1)} fusion(bf16[2,512,4,64]{1,3,2,0:T(8,128)(2,1)} %get-tuple-element.492, s32[]{:T(128)S(6)} %copy.112, f32[4,512,512]{1,2,0:T(8,128)} %subtract_exponential_fusion.3, f32[4,512,512]{1,2,0:T(8,128)} %fusion.230, bf16[1024,1,4,64]{0,3,2,1:T(8,128)(2,1)} %copy-done.4, s32[]{:T(128)S(6)} %select_n.203), kind=kOutput, calls=%fused_computation.41.clone.1 | convolution fusion | flops 139463168 | bytes 17563656 | tf_op jit(solution)/shard_map/while/body/eval_jaxpr/hqk,khc->qhc/dot_general | solution.py:101
  293.6 3.7 fusion.233
  302.7 2.8 fusion.230
  305.4 3.3 subtract_exponential_fusion.3
  308.7 7.9 %fusion.232 = bf16[2,512,4,64]{1,3,2,0:T(8,128)(2,1)} fusion(bf16[2,512,4,64]{1,3,2,0:T(8,128)(2,1)} %get-tuple-element.493, s32[]{:T(128)S(6)} %copy.112, f32[4,512,512]{1,2,0:T(8,128)} %subtract_exponential_fusion.3, f32[4,512,512]{1,2,0:T(8,128)} %fusion.230, bf16[1024,1,4,64]{0,3,2,1:T(8,128)(2,1)} %copy-done.5, s32[]{:T(128)S(6)} %select_n.203), kind=kOutput, calls=%fused_computation.43.clone.1 | convolution fusion | flops 139463168 | bytes 17563656 | tf_op jit(solution)/shard_map/while/body/eval_jaxpr/hqk,qhc->khc/dot_general | solution.py:102
  316.6 8.0 %fusion.231 = bf16[2,512,4,64]{1,3,2,0:T(8,128)(2,1)} fusion(bf16[2,512,4,64]{1,3,2,0:T(8,128)(2,1)} %get-tuple-element.492, s32[]{:T(128)S(6)} %copy.112, f32[4,512,512]{1,2,0:T(8,128)} %subtract_exponential_fusion.3, f32[4,512,512]{1,2,0:T(8,128)} %fusion.230, bf16[1024,1,4,64]{0,3,2,1:T(8,128)(2,1)} %copy-done.4, s32[]{:T(128)S(6)} %select_n.203), kind=kOutput, calls=%fused_computation.41.clone.1 | convolution fusion | flops 139463168 | bytes 17563656 | tf_op jit(solution)/shard_map/while/body/eval_jaxpr/hqk,khc->qhc/dot_general | solution.py:101
  324.6 3.7 fusion.233
  328.3 2.4 copy.85
  330.6 3.9 reshape.388
  334.5 2.3 copy.83
  336.9 4.8 reshape.386
  343.0 4.8 reshape.387
  347.8 5.8 pad_maximum_fusion.2
  353.6 10.2 %gather_fusion.3 = bf16[1024,3,256]{2,1,0:T(4,128)(2,1)} fusion(bf16[1024,3,256]{2,1,0:T(4,128)(2,1)} %pad_maximum_fusion.2, s32[1024]{0:T(1024)S(1)} %copy-done.40), kind=kCustom, calls=%fused_computation.1.clone | custom fusion | bytes 3149824 | tf_op jit(solution)/shard_map/jit(_take)/gather | solution.py:290
  363.8 5.3 broadcast_select_fusion
  371.9 5.7 bitcast_convert_fusion
  377.7 1.9 fusion.122
  379.6 1.9 fusion.119
  381.6 2.0 fusion.132
  383.6 2.3 fusion.95
  386.0 61.0 %all-reduce.7.cloned.1.call-done = (bf16[128,3,256]{2,0,1:T(8,128)(2,1)}, bf16[256,128]{1,0:T(8,128)(2,1)}, bf16[128,1024]{1,0:T(8,128)(2,1)}, bf16[1024,128]{1,0:T(8,128)(2,1)}) async-done(((bf16[128,3,256]{2,0,1:T(8,128)(2,1)}, bf16[256,128]{1,0:T(8,128)(2,1)}, bf16[128,1024]{1,0:T(8,128)(2,1)}, bf16[1024,128]{1,0:T(8,128)(2,1)}), (bf16[128,3,256]{2,0,1:T(8,128)(2,1)}, bf16[256,128]{1,0:T(8,128)(2,1)}, ...) | async-done | bytes 786448 | tf_op jit(solution)/shard_map/psum | solution.py:314
  450.2 1.8 convert_element_type.148
  451.9 1.8 convert_element_type.150
  453.7 27.9 %reduce-scatter.11.cloned.1.call-done = bf16[256,1152]{1,0:T(8,128)(2,1)} async-done(((bf16[1024,1152]{1,0:T(8,128)(2,1)}), bf16[256,1152]{1,0:T(8,128)(2,1)}) %reduce-scatter.11.cloned.1.call-update) | async-done | bytes 589840 | tf_op jit(solution)/shard_map/reduce_scatter | solution.py:296
  489.3 134.8 %all-reduce.5.cloned.1.call-done = (f32[1024,128]{1,0:T(8,128)}, f32[128,1024]{1,0:T(8,128)}, f32[1024,128]{1,0:T(8,128)}, f32[128,1024]{1,0:T(8,128)}) async-done(((f32[1024,128]{1,0:T(8,128)}, f32[128,1024]{1,0:T(8,128)}, f32[1024,128]{1,0:T(8,128)}, f32[128,1024]{1,0:T(8,128)}), (f32[1024,128]{1,0:T(8,128)}, f32[128,1024]{1,0:T(8,128)}, f32[1024,128]{1,0:T(8,128)}, ...) | async-done | bytes 2097168 | tf_op jit(solution)/shard_map/psum | solution.py:309
  624.1 1.9 copy.137
  626.0 1.9 copy.138
  627.9 1.9 copy.139
  629.7 1.9 copy.140
  (261 shorter events, 63.9 us)
Async XLA Ops:
  7.2 148.1 %copy-start = (bf16[1024,128]{1,0:T(8,128)(2,1)S(1)}, bf16[1024,128]{1,0:T(8,128)(2,1)}, u32[]{:S(2)}) copy-start(bf16[1024,128]{1,0:T(8,128)(2,1)} %param.52) | copy-start | bytes 786436
  7.2 31.6 %all-gather.5.cloned.1.call-start = ((), (), s32[]{:S(2)}) async-start(), calls=%async_computation.4 | async-start | bytes 2621440 | tf_op jit(solution)/shard_map/all_gather | solution.py:196
  8.5 30.4 %copy-start.38 = (f32[256]{0:T(256)}, f32[256]{0:T(256)S(1)}, u32[]{:S(2)}) copy-start(f32[256]{0:T(256)S(1)} %broadcast_multiply_fusion.1) | copy-start | bytes 3076
  9.8 29.0 %copy-start.55 = (f32[256]{0:T(256)}, f32[256]{0:T(256)S(1)}, u32[]{:S(2)}) copy-start(f32[256]{0:T(256)S(1)} %fusion.103) | copy-start | bytes 3076
  9.8 29.0 %copy-start.46 = (f32[256]{0:T(256)}, f32[256]{0:T(256)S(1)}, u32[]{:S(2)}) copy-start(f32[256]{0:T(256)S(1)} %fusion.138) | copy-start | bytes 3076
  12.0 111.8 %reduce-scatter.5.cloned.1.call-start = ((), (), s32[]{:S(2)}) async-start(), calls=%async_computation.5 | async-start | bytes 2949120 | tf_op jit(solution)/shard_map/reduce_scatter | solution.py:207
  12.8 4.3 copy-start.44
  17.2 14.0 %copy-start.58 = (s32[128]{0:T(128)}, s32[128]{0:T(128)S(1)}, u32[]{:S(2)}) copy-start(s32[128]{0:T(128)S(1)} %and_select_fusion) | copy-start | bytes 1540
  18.5 24.1 %copy-start.36 = (s32[1024]{0:T(1024)}, s32[1024]{0:T(1024)S(1)}, u32[]{:S(2)}) copy-start(s32[1024]{0:T(1024)S(1)} %fusion.125) | copy-start | bytes 12292
  29.1 13.6 %copy-start.19 = (bf16[1024,128]{1,0:T(8,128)(2,1)}, bf16[1024,128]{1,0:T(8,128)(2,1)S(1)}, u32[]{:S(2)}) copy-start(bf16[1024,128]{1,0:T(8,128)(2,1)S(1)} %all_gather.29) | copy-start | bytes 786436
  31.2 24.9 %copy-start.49 = (pred[1024]{0:T(1024)(128)(4,1)}, pred[1024]{0:T(1024)(128)(4,1)S(1)}, u32[]{:S(2)}) copy-start(pred[1024]{0:T(1024)(128)(4,1)S(1)} %compare_and_fusion) | copy-start | bytes 3076
  31.9 10.8 %copy-start.34 = (bf16[128,3,256]{2,0,1:T(8,128)(2,1)S(1)}, bf16[128,3,256]{2,0,1:T(8,128)(2,1)}, u32[]{:S(2)}) copy-start(bf16[128,3,256]{2,0,1:T(8,128)(2,1)} %param.49) | copy-start | bytes 589828
  56.1 9.2 %copy-start.65 = (s32[1,2]{1,0:T(1,128)S(1)}, s32[1,2]{1,0:T(1,128)}, u32[]{:S(2)}) copy-start(s32[1,2]{1,0:T(1,128)} %param.33) | copy-start | bytes 28
  81.2 4.7 copy-start.29
  88.9 34.9 %copy-start.2 = (bf16[256,1024]{1,0:T(8,128)(2,1)S(1)}, bf16[256,1024]{1,0:T(8,128)(2,1)}, u32[]{:S(2)}) copy-start(bf16[256,1024]{1,0:T(8,128)(2,1)} %param.31) | copy-start | bytes 1572868
  90.6 58.1 %all-gather.9.cloned.1.call-start = ((), (), s32[]{:S(2)}) async-start(), calls=%async_computation.8 | async-start | bytes 2621440 | tf_op jit(solution)/shard_map/all_gather | solution.py:239
  91.6 81.8 %all-gather.7.cloned.1.call-start = ((), (), s32[]{:S(2)}) async-start(), calls=%async_computation.6 | async-start | bytes 2621440 | tf_op jit(solution)/shard_map/all_gather | solution.py:218
  127.5 96.4 %reduce-scatter.9.cloned.1.call-start = ((), (), s32[]{:S(2)}) async-start(), calls=%async_computation.9 | async-start | bytes 2949120 | tf_op jit(solution)/shard_map/reduce_scatter | solution.py:258
  135.4 19.9 %copy-start.15 = (bf16[256,1024]{1,0:T(8,128)(2,1)S(1)}, bf16[256,1024]{1,0:T(8,128)(2,1)}, u32[]{:S(2)}) copy-start(bf16[256,1024]{1,0:T(8,128)(2,1)} %add_convert_fusion.1) | copy-start | bytes 1572868
  161.3 16.6 %copy-start.31 = (bf16[128,1024]{1,0:T(8,128)(2,1)S(1)}, bf16[128,1024]{1,0:T(8,128)(2,1)}, u32[]{:S(2)}) copy-start(bf16[128,1024]{1,0:T(8,128)(2,1)} %param.53) | copy-start | bytes 786436
  173.4 4.6 copy-start.60
  178.0 2.9 copy-start.32
  178.0 2.9 copy-start.63
  178.0 3.9 copy-start.68
  181.8 4.6 copy-start.62
  190.7 35.7 %copy-start.57 = (f32[256]{0:T(256)S(1)}, f32[256]{0:T(256)}, u32[]{:S(2)}) copy-start(f32[256]{0:T(256)} %copy-done.56) | copy-start | bytes 3076
  190.7 35.8 %copy-start.42 = (f32[256]{0:T(256)S(1)}, f32[256]{0:T(256)}, u32[]{:S(2)}) copy-start(f32[256]{0:T(256)} %copy-done.41) | copy-start | bytes 3076
  190.7 35.8 %copy-start.54 = (f32[256]{0:T(256)S(1)}, f32[256]{0:T(256)}, u32[]{:S(2)}) copy-start(f32[256]{0:T(256)} %copy-done.53) | copy-start | bytes 3076
  190.7 63.9 %all-gather.11.cloned.1.call-start = ((), (), s32[]{:S(2)}) async-start(), calls=%async_computation.10 | async-start | bytes 2621440 | tf_op jit(solution)/shard_map/all_gather | solution.py:275
  223.9 4.0 copy-start.7
  225.1 3.8 copy-start.45
  226.4 3.2 copy-start.64
  228.9 150.7 %reduce-scatter.7.cloned.1.call-start = ((), (), s32[]{:S(2)}) async-start(), calls=%async_computation.7 | async-start | bytes 2949120 | tf_op jit(solution)/shard_map/reduce_scatter | solution.py:227
  240.9 4.9 copy-start.12
  240.9 4.9 copy-start.26
  245.7 201.2 %all-reduce.7.cloned.1.call-start = ((), (), s32[]{:S(2)}) async-start(), calls=%async_computation.13 | async-start | bytes 1572864 | tf_op jit(solution)/shard_map/psum | solution.py:314
  257.3 7.6 %copy-start.50 = (pred[1024]{0:T(1024)(128)(4,1)S(1)}, pred[1024]{0:T(1024)(128)(4,1)}, u32[]{:S(2)}) copy-start(pred[1024]{0:T(1024)(128)(4,1)} %copy-done.49) | copy-start | bytes 3076
  266.1 5.1 copy-start.66
  285.6 11.7 %copy-start.67 = (s32[2]{0:T(128)S(1)}, s32[2]{0:T(128)}, u32[]{:S(2)}) copy-start(s32[2]{0:T(128)} %copy-done.66) | copy-start | bytes 28 | tf_op jit(solution)/shard_map/while
  297.2 5.1 copy-start.66
  302.6 2.8 copy-start.4
  316.6 11.7 %copy-start.67 = (s32[2]{0:T(128)S(1)}, s32[2]{0:T(128)}, u32[]{:S(2)}) copy-start(s32[2]{0:T(128)} %copy-done.66) | copy-start | bytes 28 | tf_op jit(solution)/shard_map/while
  328.3 13.4 %copy-start.30 = (bf16[2,512,4,64]{1,3,2,0:T(8,128)(2,1)S(1)}, bf16[2,512,4,64]{1,3,2,0:T(8,128)(2,1)}, u32[]{:S(2)}) copy-start(bf16[2,512,4,64]{1,3,2,0:T(8,128)(2,1)} %get-tuple-element.261) | copy-start | bytes 1572868
  341.6 12.0 %copy-start.40 = (s32[1024]{0:T(1024)S(1)}, s32[1024]{0:T(1024)}, u32[]{:S(2)}) copy-start(s32[1024]{0:T(1024)} %get-tuple-element.326) | copy-start | bytes 12292
  347.8 16.0 %copy-start.48 = (pred[1024]{0:T(1024)(128)(4,1)S(1)}, pred[1024]{0:T(1024)(128)(4,1)}, u32[]{:S(2)}) copy-start(pred[1024]{0:T(1024)(128)(4,1)} %compare_and_fusion.1) | copy-start | bytes 3076
  353.6 16.8 %copy-start.20 = (bf16[1024,128]{1,0:T(8,128)(2,1)S(1)}, bf16[1024,128]{1,0:T(8,128)(2,1)}, u32[]{:S(2)}) copy-start(bf16[1024,128]{1,0:T(8,128)(2,1)} %copy-done.19) | copy-start | bytes 786436
  363.8 8.1 %copy-start.35 = (bf16[128,3,256]{2,0,1:T(8,128)(2,1)S(1)}, bf16[128,3,256]{2,0,1:T(8,128)(2,1)}, u32[]{:S(2)}) copy-start(bf16[128,3,256]{2,0,1:T(8,128)(2,1)} %param.49) | copy-start | bytes 589828
  371.5 6.1 copy-start.13
  371.6 8.1 %copy-start.11 = (bf16[256,1024]{1,0:T(8,128)(2,1)S(1)}, bf16[256,1024]{1,0:T(8,128)(2,1)}, u32[]{:S(2)}) copy-start(bf16[256,1024]{1,0:T(8,128)(2,1)} %convert_element_type.131) | copy-start | bytes 1572868
  371.6 110.1 %reduce-scatter.11.cloned.1.call-start = ((), (), s32[]{:S(2)}) async-start(), calls=%async_computation.11 | async-start | bytes 2949120 | tf_op jit(solution)/shard_map/reduce_scatter | solution.py:296
  377.6 4.0 copy-start.16
  377.6 6.0 copy-start.27
  377.6 6.0 copy-start.61
  377.6 246.5 %all-reduce.5.cloned.1.call-start = ((), (), s32[]{:S(2)}) async-start(), calls=%async_computation.12 | async-start | bytes 4194304 | tf_op jit(solution)/shard_map/psum | solution.py:309
  379.6 104.2 %copy-start.14 = (bf16[256,1024]{1,0:T(8,128)(2,1)S(1)}, bf16[256,1024]{1,0:T(8,128)(2,1)}, u32[]{:S(2)}) copy-start(bf16[256,1024]{1,0:T(8,128)(2,1)} %fusion.106) | copy-start | bytes 1572868
  386.0 99.1 %copy-start.3 = (bf16[256,1024]{1,0:T(8,128)(2,1)S(1)}, bf16[256,1024]{1,0:T(8,128)(2,1)}, u32[]{:S(2)}) copy-start(bf16[256,1024]{1,0:T(8,128)(2,1)} %param.31) | copy-start | bytes 1572868
  386.0 99.1 %copy-start.28 = (bf16[1024,128]{1,0:T(8,128)(2,1)S(1)}, bf16[1024,128]{1,0:T(8,128)(2,1)}, u32[]{:S(2)}) copy-start(bf16[1024,128]{1,0:T(8,128)(2,1)} %param.48) | copy-start | bytes 786436
  386.0 99.1 %copy-start.39 = (f32[256]{0:T(256)S(1)}, f32[256]{0:T(256)}, u32[]{:S(2)}) copy-start(f32[256]{0:T(256)} %copy-done.38) | copy-start | bytes 3076
  386.0 99.1 %copy-start.43 = (f32[1024]{0:T(1024)S(1)}, f32[1024]{0:T(1024)}, u32[]{:S(2)}) copy-start(f32[1024]{0:T(1024)} %param.36) | copy-start | bytes 12292
  450.2 37.3 %copy-start.47 = (f32[256]{0:T(256)S(1)}, f32[256]{0:T(256)}, u32[]{:S(2)}) copy-start(f32[256]{0:T(256)} %copy-done.46) | copy-start | bytes 3076
  453.7 34.1 %copy-start.8 = (f32[256,1024]{1,0:T(8,128)S(1)}, f32[256,1024]{1,0:T(8,128)}, u32[]{:S(2)}) copy-start(f32[256,1024]{1,0:T(8,128)} %param.32) | copy-start | bytes 3145732
  453.7 34.1 %copy-start.10 = (f32[256,1024]{1,0:T(8,128)S(1)}, f32[256,1024]{1,0:T(8,128)}, u32[]{:S(2)}) copy-start(f32[256,1024]{1,0:T(8,128)} %copy-done.9) | copy-start | bytes 3145732
  453.7 34.1 %copy-start.52 = (f32[256]{0:T(256)S(1)}, f32[256]{0:T(256)}, u32[]{:S(2)}) copy-start(f32[256]{0:T(256)} %copy-done.51) | copy-start | bytes 3076
  487.8 143.8 %copy-start.1 = (bf16[1024,128]{1,0:T(8,128)(2,1)S(1)}, bf16[1024,128]{1,0:T(8,128)(2,1)}, u32[]{:S(2)}) copy-start(bf16[1024,128]{1,0:T(8,128)(2,1)} %param.52) | copy-start | bytes 786436
  (19 other events, 35.3 us)
Sparse Core Ops, SparseCore 0:
  12.1 26.6 all-gather.4
  90.7 33.0 reduce-scatter.4
  126.0 22.5 all-gather.8
  150.7 22.5 all-gather.6
  190.8 33.0 reduce-scatter.8
  229.0 23.5 all-gather.10
  255.1 33.1 reduce-scatter.6
  371.7 75.2 all-reduce.6
  449.5 32.0 reduce-scatter.10
  489.2 134.8 all-reduce.4
where the time goes:
time: 643 us; the launch traced here: 639 us
  waiting for transfers between devices  321 us (50%)
  matrix products  123 us (19%)
  local copies, waits for them, and re-layouts  87.2 us (14%)
  other arithmetic  53.3 us (8%)
  blocking collectives  27.4 us (4%)
  between operations  15.3 us (2%)
  loops' own time  10.6 us (2%)
    psum x1, waiting for transfers between devices, body(): lax.psum((grad_qkv_in_part, grad_proj_out_part, grad_up_in_part, grad_dow...  135 us
    reduce_scatter x2, waiting for transfers between devices, body(): lax.psum_scatter(jnp.concatenate([part[:, :D], part[:, D:]], 1).astype(jn...  61 us
    psum x1, waiting for transfers between devices, body(): lax.psum(grad_qkv_out_part.astype(jnp.bfloat16), 'dp').astype(jnp.float32)  61 us
    reduce_scatter x2, waiting for transfers between devices, body(): lax.psum_scatter(jnp.concatenate([part[:, :D], part[:, D:] * mask_rows],...  32.2 us
    dot_general x9, matrix products, matmul_back(): lax.dot_general(left, right, (((1,), (1,)), ((), ())), preferred_element_...  21.5 us
    another operation x6, local copies, waits for them, and re-layouts, attention_backward(): return jnp.stack([grad_query, grad_key, grad_value], 1)  19.6 us
    dot_general x8, matrix products, matmul(): return jnp.dot(left, right, preferred_element_type=jnp.float32)  19.2 us
    unnamed x134, local copies, waits for them, and re-layouts  17.1 us
  transfers between devices with their start and end apart: 10, of which 8 were waited for; matrix products, arithmetic and copies ran while one was open for 28% of the time, Pallas kernels for 0%

commit v1 on v0

--- a/solution.py
+++ b/solution.py
@@ -311,7 +311,9 @@
         ("dp", "tensor"),
     )
     narrow = (
-        lax.psum(grad_qkv_out_part.astype(jnp.bfloat16), "dp").astype(jnp.float32),
+        jnp.sum(lax.all_gather(grad_qkv_out_part.astype(jnp.bfloat16), "dp"), axis=0).astype(
+            jnp.float32
+        ),
         lax.psum(grad_proj_in_part.astype(jnp.bfloat16), "dp").astype(jnp.float32),
         lax.psum(grad_up_out_part.astype(jnp.bfloat16), "dp").astype(jnp.float32),
         lax.psum(grad_down_in_part.astype(jnp.bfloat16), "dp").astype(jnp.float32),

time: 643 us -> 612 us (0.952)
  waiting for transfers between devices: 321 us -> 289 us
    psum x1, waiting for transfers between devices: 61 us -> 0.01 us  [body(): lax.psum(grad_proj_in_part.astype(jnp.bfloat16), 'dp').astype(jnp.float32)]
    all_gather x0 -> x1, waiting for transfers between devices: none -> 24.8 us  [body(): lax.all_gather(grad_qkv_out_part.astype(jnp.bfloat16), 'dp')]
    unnamed x134 -> x132, local copies, waits for them, and re-layouts: 17.1 us -> 16 us
  transfers between devices with their start and end apart: 10 -> 11, of which waited for: 8 -> 8; matrix products, arithmetic and copies ran while one was open for 28% -> 29% of each run, Pallas kernels for 0% -> 0%
where the time goes in v1:
time: 612 us; the launch traced here: 607 us
  waiting for transfers between devices  289 us (47%)
  matrix products  124 us (20%)
  local copies, waits for them, and re-layouts  86.1 us (14%)
  other arithmetic  54.2 us (9%)
  blocking collectives  26.9 us (4%)
  between operations  15 us (2%)
  loops' own time  10.6 us (2%)
    psum x1, waiting for transfers between devices, body(): lax.psum((grad_qkv_in_part, grad_proj_out_part, grad_up_in_part, grad_dow...  135 us
    reduce_scatter x2, waiting for transfers between devices, body(): lax.psum_scatter(jnp.concatenate([part[:, :D], part[:, D:]], 1).astype(jn...  65 us
    reduce_scatter x2, waiting for transfers between devices, body(): lax.psum_scatter(jnp.concatenate([part[:, :D], part[:, D:] * mask_rows],...  32.2 us
    all_gather x1, waiting for transfers between devices, body(): lax.all_gather(grad_qkv_out_part.astype(jnp.bfloat16), 'dp')  24.8 us
    dot_general x9, matrix products, matmul_back(): lax.dot_general(left, right, (((1,), (1,)), ((), ())), preferred_element_...  22.2 us
    another operation x6, local copies, waits for them, and re-layouts, attention_backward(): return jnp.stack([grad_query, grad_key, grad_value], 1)  19.6 us
    dot_general x8, matrix products, matmul(): return jnp.dot(left, right, preferred_element_type=jnp.float32)  19.3 us
    dot_general x2, matrix products, one_block(): jnp.einsum('hqk,khc->qhc', grad_raw, keys, preferred_element_type=jnp.flo...  16 us
  transfers between devices with their start and end apart: 11, of which 8 were waited for; matrix products, arithmetic and copies ran while one was open for 29% of the time, Pallas kernels for 0%

profile of v1, /device:TPU:0, one launch (start us, length us, event | category | flops | bytes accessed | tf_op | source)
XLA Modules:
  0.0 607.1 jit_solution(16322936307228219762)
XLA Ops:
  9.8 2.1 fusion.106
  12.8 4.3 scatter_custom_fusion
  20.1 8.9 %all_gather.35 = bf16[1024,128]{1,0:T(8,128)(2,1)S(1)} all-gather(bf16[256,128]{1,0:T(8,128)(2,1)S(1)} %fusion.97), channel_id=1, replica_groups=mesh['dp'=8,'tensor'=4] {'tensor'}, dimensions={0}, use_global_device_ids=true | all-gather | bytes 327680 | tf_op jit(solution)/shard_map/all_gather | solution.py:197
  31.9 6.9 %all-gather.7.cloned.1.call-done = bf16[1024,1024]{1,0:T(8,128)(2,1)} async-done(((bf16[256,1024]{1,0:T(8,128)(2,1)}), bf16[1024,1024]{1,0:T(8,128)(2,1)}) %all-gather.7.cloned.1.call-update) | async-done | bytes 2097168 | tf_op jit(solution)/shard_map/all_gather | solution.py:196
  38.8 3.8 fusion.84
  43.3 2.8 copy.65
  46.0 10.1 %gather_fusion.2 = bf16[1024,3,256]{2,1,0:T(4,128)(2,1)} fusion(bf16[1024,3,256]{2,1,0:T(4,128)(2,1)} %copy.65, s32[1024]{0:T(1024)S(1)} %fusion.129), kind=kCustom, calls=%fused_computation.clone | custom fusion | bytes 3149824 | tf_op jit(solution)/shard_map/jit(_take)/gather | solution.py:201
  56.2 6.3 %broadcast_select_fusion.1 = bf16[1024,3,256]{2,1,0:T(4,128)(2,1)} fusion(bf16[1024,3,256]{2,1,0:T(4,128)(2,1)} %gather_fusion.2, pred[1024]{0:T(1024)(128)(4,1)S(1)} %compare_and_fusion), kind=kLoop, calls=%fused_computation.99 | loop fusion | flops 786432 | bytes 3146752 | tf_op jit(solution)/shard_map/jit(_take)/select_n | solution.py:201
  62.5 2.9 copy.66
  65.4 15.9 %while.32 = (s32[]{:T(128)}, bf16[2,512,256]{1,2,0:T(8,128)(2,1)S(1)}, f32[2,4,512]{2,1,0:T(4,128)S(1)}, bf16[1024,3,4,64]{0,3,2,1:T(8,128)(2,1)S(1)}, s32[2]{0:...) while((s32[]{:T(128)}, ...), condition=%wide.region_7.9_spmd, body=%wide.region_4.8_spmd.sunk | while | flops 281541120 | bytes 18417900 | solution.py:72
  81.5 4.4 gather_fusion
  86.0 1.8 fusion.108
  91.8 32.2 %reduce-scatter.5.cloned.1.call-done = bf16[256,1152]{1,0:T(8,128)(2,1)} async-done(((bf16[1024,1152]{1,0:T(8,128)(2,1)}), bf16[256,1152]{1,0:T(8,128)(2,1)}) %reduce-scatter.5.cloned.1.call-update) | async-done | bytes 589840 | tf_op jit(solution)/shard_map/reduce_scatter | solution.py:207
  125.8 1.8 add_convert_fusion.1
  129.1 6.4 %all_gather.39 = bf16[1024,128]{1,0:T(8,128)(2,1)} all-gather(bf16[256,128]{1,0:T(8,128)(2,1)S(1)} %fusion.99), channel_id=1, replica_groups=mesh['dp'=8,'tensor'=4] {'tensor'}, dimensions={0}, use_global_device_ids=true | all-gather | bytes 327680 | tf_op jit(solution)/shard_map/all_gather | solution.py:240
  135.5 13.3 %all-gather.11.cloned.1.call-done = bf16[1024,1024]{1,0:T(8,128)(2,1)} async-done(((bf16[256,1024]{1,0:T(8,128)(2,1)}), bf16[1024,1024]{1,0:T(8,128)(2,1)}) %all-gather.11.cloned.1.call-update) | async-done | bytes 2097168 | tf_op jit(solution)/shard_map/all_gather | solution.py:239
  148.8 6.5 %fusion.153 = f32[1024,1024]{1,0:T(8,128)} fusion(bf16[1024,1024]{1,0:T(8,128)(2,1)} %all-gather.11.cloned.1.call-done, bf16[1024,1024]{1,0:T(8,128)(2,1)} %param.46), kind=kOutput, calls=%fused_computation.219 | convolution fusion | flops 2147483648 | bytes 8388608 | tf_op jit(solution)/shard_map/dot_general | solution.py:25
  155.6 5.8 all_gather.37
  161.4 12.1 %all-gather.9.cloned.1.call-done = bf16[1024,1024]{1,0:T(8,128)(2,1)} async-done(((bf16[256,1024]{1,0:T(8,128)(2,1)}), bf16[1024,1024]{1,0:T(8,128)(2,1)}) %all-gather.9.cloned.1.call-update) | async-done | bytes 2097168 | tf_op jit(solution)/shard_map/all_gather | solution.py:218
  173.5 4.6 fusion.152
  178.8 2.1 copy-done.18
  182.0 3.2 fusion.76
  186.5 4.2 convolution_convert_fusion
  190.8 33.1 %reduce-scatter.9.cloned.1.call-done = bf16[256,1152]{1,0:T(8,128)(2,1)} async-done(((bf16[1024,1152]{1,0:T(8,128)(2,1)}), bf16[256,1152]{1,0:T(8,128)(2,1)}) %reduce-scatter.9.cloned.1.call-update) | async-done | bytes 589840 | tf_op jit(solution)/shard_map/reduce_scatter | solution.py:258
  228.9 6.6 %fusion.77 = bf16[1024,1152]{1,0:T(8,128)(2,1)S(1)} fusion(bf16[1024,128]{1,0:T(8,128)(2,1)} %param.54, bf16[1024,1024]{1,0:T(8,128)(2,1)} %param.46, f32[1024,1024]{1,0:T(8,128)} %copy-done.18), kind=kOutput, calls=%fused_computation.87 | convolution fusion | flops 2430074880 | bytes 8912896 | tf_op jit(solution)/shard_map/dot_general | solution.py:21
  238.8 2.8 convolution_convert_fusion.2
  241.6 4.8 convolution_convert_fusion.1
  246.7 5.8 all_gather.41
  253.8 2.4 fusion.154
  257.4 5.5 gather_fusion.1
  262.9 2.1 copy.68
  266.1 61.9 %while.33 = (s32[]{:T(128)}, bf16[2,512,4,64]{1,3,2,0:T(8,128)(2,1)}, bf16[2,512,4,64]{1,3,2,0:T(8,128)(2,1)}, bf16[2,512,4,64]{1,3,2,0:T(8,128)(2,1)}, bf16[102...) while((s32[]{:T(128)}, ...), condition=%wide.region_17.19_spmd, body=%wide.region_15.18_spmd.sunk | while | flops 686298624 | bytes 57437636 | solution.py:112
  271.6 2.7 fusion.230
  274.3 3.2 subtract_exponential_fusion.3
  277.5 7.9 %fusion.232 = bf16[2,512,4,64]{1,3,2,0:T(8,128)(2,1)} fusion(bf16[2,512,4,64]{1,3,2,0:T(8,128)(2,1)} %get-tuple-element.492, s32[]{:T(128)S(6)} %copy.112, f32[4,512,512]{1,2,0:T(8,128)} %subtract_exponential_fusion.3, f32[4,512,512]{1,2,0:T(8,128)} %fusion.230, bf16[1024,1,4,64]{0,3,2,1:T(8,128)(2,1)} %copy-done.5, s32[]{:T(128)S(6)} %select_n.203), kind=kOutput, calls=%fused_computation.43.clone.1 | convolution fusion | flops 139463168 | bytes 17563656 | tf_op jit(solution)/shard_map/while/body/eval_jaxpr/hqk,qhc->khc/dot_general | solution.py:102
  285.5 8.0 %fusion.231 = bf16[2,512,4,64]{1,3,2,0:T(8,128)(2,1)} fusion(bf16[2,512,4,64]{1,3,2,0:T(8,128)(2,1)} %get-tuple-element.491, s32[]{:T(128)S(6)} %copy.112, f32[4,512,512]{1,2,0:T(8,128)} %subtract_exponential_fusion.3, f32[4,512,512]{1,2,0:T(8,128)} %fusion.230, bf16[1024,1,4,64]{0,3,2,1:T(8,128)(2,1)} %copy-done.4, s32[]{:T(128)S(6)} %select_n.203), kind=kOutput, calls=%fused_computation.41.clone.1 | convolution fusion | flops 139463168 | bytes 17563656 | tf_op jit(solution)/shard_map/while/body/eval_jaxpr/hqk,khc->qhc/dot_general | solution.py:101
  293.5 3.7 fusion.233
  302.6 2.7 fusion.230
  305.3 3.3 subtract_exponential_fusion.3
  308.5 7.9 %fusion.232 = bf16[2,512,4,64]{1,3,2,0:T(8,128)(2,1)} fusion(bf16[2,512,4,64]{1,3,2,0:T(8,128)(2,1)} %get-tuple-element.492, s32[]{:T(128)S(6)} %copy.112, f32[4,512,512]{1,2,0:T(8,128)} %subtract_exponential_fusion.3, f32[4,512,512]{1,2,0:T(8,128)} %fusion.230, bf16[1024,1,4,64]{0,3,2,1:T(8,128)(2,1)} %copy-done.5, s32[]{:T(128)S(6)} %select_n.203), kind=kOutput, calls=%fused_computation.43.clone.1 | convolution fusion | flops 139463168 | bytes 17563656 | tf_op jit(solution)/shard_map/while/body/eval_jaxpr/hqk,qhc->khc/dot_general | solution.py:102
  316.4 8.0 %fusion.231 = bf16[2,512,4,64]{1,3,2,0:T(8,128)(2,1)} fusion(bf16[2,512,4,64]{1,3,2,0:T(8,128)(2,1)} %get-tuple-element.491, s32[]{:T(128)S(6)} %copy.112, f32[4,512,512]{1,2,0:T(8,128)} %subtract_exponential_fusion.3, f32[4,512,512]{1,2,0:T(8,128)} %fusion.230, bf16[1024,1,4,64]{0,3,2,1:T(8,128)(2,1)} %copy-done.4, s32[]{:T(128)S(6)} %select_n.203), kind=kOutput, calls=%fused_computation.41.clone.1 | convolution fusion | flops 139463168 | bytes 17563656 | tf_op jit(solution)/shard_map/while/body/eval_jaxpr/hqk,khc->qhc/dot_general | solution.py:101
  324.4 3.7 fusion.233
  328.0 2.4 copy.85
  330.4 3.9 reshape.389
  334.3 2.3 copy.83
  336.6 4.8 reshape.387
  342.8 4.8 reshape.388
  347.6 5.8 pad_maximum_fusion.2
  353.4 10.2 %gather_fusion.3 = bf16[1024,3,256]{2,1,0:T(4,128)(2,1)} fusion(bf16[1024,3,256]{2,1,0:T(4,128)(2,1)} %pad_maximum_fusion.2, s32[1024]{0:T(1024)S(1)} %copy-done.39), kind=kCustom, calls=%fused_computation.1.clone | custom fusion | bytes 3149824 | tf_op jit(solution)/shard_map/jit(_take)/gather | solution.py:290
  363.6 5.3 broadcast_select_fusion
  371.7 5.7 bitcast_convert_fusion
  377.6 1.9 fusion.122
  379.5 1.9 fusion.119
  381.4 2.0 fusion.132
  383.5 2.4 fusion.95
  387.4 1.8 convert_element_type.150
  389.2 1.9 convert_element_type.152
  391.0 24.8 %all-gather.15.cloned.1.call-done = bf16[1024,3,256]{2,0,1:T(8,128)(2,1)} async-done(((bf16[128,3,256]{2,0,1:T(8,128)(2,1)}), bf16[1024,3,256]{2,0,1:T(8,128)(2,1)}) %all-gather.15.cloned.1.call-update) | async-done | bytes 1572880 | tf_op jit(solution)/shard_map/all_gather | solution.py:314
  418.3 31.8 %reduce-scatter.11.cloned.1.call-done = bf16[256,1152]{1,0:T(8,128)(2,1)} async-done(((bf16[1024,1152]{1,0:T(8,128)(2,1)}), bf16[256,1152]{1,0:T(8,128)(2,1)}) %reduce-scatter.11.cloned.1.call-update) | async-done | bytes 589840 | tf_op jit(solution)/shard_map/reduce_scatter | solution.py:296
  457.8 135.0 %all-reduce.5.cloned.1.call-done = (f32[1024,128]{1,0:T(8,128)}, f32[128,1024]{1,0:T(8,128)}, f32[1024,128]{1,0:T(8,128)}, f32[128,1024]{1,0:T(8,128)}) async-done(((f32[1024,128]{1,0:T(8,128)}, f32[128,1024]{1,0:T(8,128)}, f32[1024,128]{1,0:T(8,128)}, f32[128,1024]{1,0:T(8,128)}), (f32[1024,128]{1,0:T(8,128)}, f32[128,1024]{1,0:T(8,128)}, f32[1024,128]{1,0:T(8,128)}, ...) | async-done | bytes 2097168 | tf_op jit(solution)/shard_map/psum | solution.py:309
  592.8 1.9 copy.136
  594.6 1.9 copy.137
  596.5 1.9 copy.138
  598.4 1.9 copy.139
  (263 shorter events, 64.5 us)
Async XLA Ops:
  7.2 148.2 %copy-start = (bf16[1024,128]{1,0:T(8,128)(2,1)S(1)}, bf16[1024,128]{1,0:T(8,128)(2,1)}, u32[]{:S(2)}) copy-start(bf16[1024,128]{1,0:T(8,128)(2,1)} %param.52) | copy-start | bytes 786436
  7.2 31.6 %all-gather.7.cloned.1.call-start = ((), (), s32[]{:S(2)}) async-start(), calls=%async_computation.4 | async-start | bytes 2621440 | tf_op jit(solution)/shard_map/all_gather | solution.py:196
  8.5 30.4 %copy-start.37 = (f32[256]{0:T(256)}, f32[256]{0:T(256)S(1)}, u32[]{:S(2)}) copy-start(f32[256]{0:T(256)S(1)} %broadcast_multiply_fusion.1) | copy-start | bytes 3076
  9.8 29.0 %copy-start.55 = (f32[256]{0:T(256)}, f32[256]{0:T(256)S(1)}, u32[]{:S(2)}) copy-start(f32[256]{0:T(256)S(1)} %fusion.103) | copy-start | bytes 3076
  9.8 29.0 %copy-start.45 = (f32[256]{0:T(256)}, f32[256]{0:T(256)S(1)}, u32[]{:S(2)}) copy-start(f32[256]{0:T(256)S(1)} %fusion.138) | copy-start | bytes 3076
  12.0 112.0 %reduce-scatter.5.cloned.1.call-start = ((), (), s32[]{:S(2)}) async-start(), calls=%async_computation.5 | async-start | bytes 2949120 | tf_op jit(solution)/shard_map/reduce_scatter | solution.py:207
  12.8 4.3 copy-start.43
  17.2 14.0 %copy-start.58 = (s32[128]{0:T(128)}, s32[128]{0:T(128)S(1)}, u32[]{:S(2)}) copy-start(s32[128]{0:T(128)S(1)} %and_select_fusion) | copy-start | bytes 1540
  18.5 24.2 %copy-start.35 = (s32[1024]{0:T(1024)}, s32[1024]{0:T(1024)S(1)}, u32[]{:S(2)}) copy-start(s32[1024]{0:T(1024)S(1)} %fusion.125) | copy-start | bytes 12292
  29.1 13.6 %copy-start.19 = (bf16[1024,128]{1,0:T(8,128)(2,1)}, bf16[1024,128]{1,0:T(8,128)(2,1)S(1)}, u32[]{:S(2)}) copy-start(bf16[1024,128]{1,0:T(8,128)(2,1)S(1)} %all_gather.35) | copy-start | bytes 786436
  31.2 25.0 %copy-start.49 = (pred[1024]{0:T(1024)(128)(4,1)}, pred[1024]{0:T(1024)(128)(4,1)S(1)}, u32[]{:S(2)}) copy-start(pred[1024]{0:T(1024)(128)(4,1)S(1)} %compare_and_fusion) | copy-start | bytes 3076
  31.9 10.8 %copy-start.33 = (bf16[128,3,256]{2,0,1:T(8,128)(2,1)S(1)}, bf16[128,3,256]{2,0,1:T(8,128)(2,1)}, u32[]{:S(2)}) copy-start(bf16[128,3,256]{2,0,1:T(8,128)(2,1)} %param.49) | copy-start | bytes 589828
  56.2 9.2 %copy-start.64 = (s32[1,2]{1,0:T(1,128)S(1)}, s32[1,2]{1,0:T(1,128)}, u32[]{:S(2)}) copy-start(s32[1,2]{1,0:T(1,128)} %param.33) | copy-start | bytes 28
  81.3 4.7 copy-start.29
  89.0 34.9 %copy-start.2 = (bf16[256,1024]{1,0:T(8,128)(2,1)S(1)}, bf16[256,1024]{1,0:T(8,128)(2,1)}, u32[]{:S(2)}) copy-start(bf16[256,1024]{1,0:T(8,128)(2,1)} %param.31) | copy-start | bytes 1572868
  90.8 58.0 %all-gather.11.cloned.1.call-start = ((), (), s32[]{:S(2)}) async-start(), calls=%async_computation.8 | async-start | bytes 2621440 | tf_op jit(solution)/shard_map/all_gather | solution.py:239
  91.7 81.8 %all-gather.9.cloned.1.call-start = ((), (), s32[]{:S(2)}) async-start(), calls=%async_computation.6 | async-start | bytes 2621440 | tf_op jit(solution)/shard_map/all_gather | solution.py:218
  127.6 96.3 %reduce-scatter.9.cloned.1.call-start = ((), (), s32[]{:S(2)}) async-start(), calls=%async_computation.9 | async-start | bytes 2949120 | tf_op jit(solution)/shard_map/reduce_scatter | solution.py:258
  135.5 19.8 %copy-start.15 = (bf16[256,1024]{1,0:T(8,128)(2,1)S(1)}, bf16[256,1024]{1,0:T(8,128)(2,1)}, u32[]{:S(2)}) copy-start(bf16[256,1024]{1,0:T(8,128)(2,1)} %add_convert_fusion.1) | copy-start | bytes 1572868
  161.4 16.6 %copy-start.31 = (bf16[128,1024]{1,0:T(8,128)(2,1)S(1)}, bf16[128,1024]{1,0:T(8,128)(2,1)}, u32[]{:S(2)}) copy-start(bf16[128,1024]{1,0:T(8,128)(2,1)} %param.53) | copy-start | bytes 786436
  173.5 4.6 copy-start.60
  178.1 2.9 copy-start.32
  178.1 3.9 copy-start.67
  182.0 4.6 copy-start.62
  190.7 35.7 %copy-start.57 = (f32[256]{0:T(256)S(1)}, f32[256]{0:T(256)}, u32[]{:S(2)}) copy-start(f32[256]{0:T(256)} %copy-done.56) | copy-start | bytes 3076
  190.7 35.7 %copy-start.41 = (f32[256]{0:T(256)S(1)}, f32[256]{0:T(256)}, u32[]{:S(2)}) copy-start(f32[256]{0:T(256)} %copy-done.40) | copy-start | bytes 3076
  190.7 35.7 %copy-start.54 = (f32[256]{0:T(256)S(1)}, f32[256]{0:T(256)}, u32[]{:S(2)}) copy-start(f32[256]{0:T(256)} %copy-done.53) | copy-start | bytes 3076
  190.8 63.1 %all-gather.13.cloned.1.call-start = ((), (), s32[]{:S(2)}) async-start(), calls=%async_computation.10 | async-start | bytes 2621440 | tf_op jit(solution)/shard_map/all_gather | solution.py:275
  224.0 3.9 copy-start.7
  226.9 8.7 %copy-start.51 = (f32[256]{0:T(256)}, f32[256]{0:T(256)S(1)}, u32[]{:S(2)}) copy-start(f32[256]{0:T(256)S(1)} %negate_multiply_fusion.1) | copy-start | bytes 3076
  228.9 150.6 %reduce-scatter.7.cloned.1.call-start = ((), (), s32[]{:S(2)}) async-start(), calls=%async_computation.7 | async-start | bytes 2949120 | tf_op jit(solution)/shard_map/reduce_scatter | solution.py:227
  238.1 147.7 %all-reduce.7.cloned.1.call-start = ((), (), s32[]{:S(2)}) async-start(), calls=%async_computation.14 | async-start | bytes 1179648 | tf_op jit(solution)/shard_map/psum | solution.py:317
  241.6 4.8 copy-start.12
  241.6 4.8 copy-start.26
  241.6 10.9 %copy-start.23 = (bf16[1024,256]{1,0:T(8,128)(2,1)S(1)}, bf16[1024,256]{1,0:T(8,128)(2,1)}, u32[]{:S(2)}) copy-start(bf16[1024,256]{1,0:T(8,128)(2,1)} %copy-done.22) | copy-start | bytes 1572868
  241.6 10.9 %copy-start.47 = (pred[1024]{0:T(1024)(128)(4,1)S(1)}, pred[1024]{0:T(1024)(128)(4,1)}, u32[]{:S(2)}) copy-start(pred[1024]{0:T(1024)(128)(4,1)} %compare_and_fusion.1) | copy-start | bytes 3076
  253.7 162.1 %all-gather.15.cloned.1.call-start = ((), (), s32[]{:S(2)}) async-start(), calls=%async_computation.12 | async-start | bytes 1769472 | tf_op jit(solution)/shard_map/all_gather | solution.py:314
  257.4 7.6 %copy-start.50 = (pred[1024]{0:T(1024)(128)(4,1)S(1)}, pred[1024]{0:T(1024)(128)(4,1)}, u32[]{:S(2)}) copy-start(pred[1024]{0:T(1024)(128)(4,1)} %copy-done.49) | copy-start | bytes 3076
  266.1 5.1 copy-start.65
  285.5 11.7 %copy-start.66 = (s32[2]{0:T(128)S(1)}, s32[2]{0:T(128)}, u32[]{:S(2)}) copy-start(s32[2]{0:T(128)} %copy-done.65) | copy-start | bytes 28 | tf_op jit(solution)/shard_map/while
  297.1 5.1 copy-start.65
  316.4 11.6 %copy-start.66 = (s32[2]{0:T(128)S(1)}, s32[2]{0:T(128)}, u32[]{:S(2)}) copy-start(s32[2]{0:T(128)} %copy-done.65) | copy-start | bytes 28 | tf_op jit(solution)/shard_map/while
  328.0 13.4 %copy-start.30 = (bf16[2,512,4,64]{1,3,2,0:T(8,128)(2,1)S(1)}, bf16[2,512,4,64]{1,3,2,0:T(8,128)(2,1)}, u32[]{:S(2)}) copy-start(bf16[2,512,4,64]{1,3,2,0:T(8,128)(2,1)} %get-tuple-element.261) | copy-start | bytes 1572868
  341.4 12.0 %copy-start.39 = (s32[1024]{0:T(1024)S(1)}, s32[1024]{0:T(1024)}, u32[]{:S(2)}) copy-start(s32[1024]{0:T(1024)} %get-tuple-element.325) | copy-start | bytes 12292
  347.6 16.0 %copy-start.48 = (pred[1024]{0:T(1024)(128)(4,1)S(1)}, pred[1024]{0:T(1024)(128)(4,1)}, u32[]{:S(2)}) copy-start(pred[1024]{0:T(1024)(128)(4,1)} %compare_and_fusion.1) | copy-start | bytes 3076
  353.4 16.9 %copy-start.20 = (bf16[1024,128]{1,0:T(8,128)(2,1)S(1)}, bf16[1024,128]{1,0:T(8,128)(2,1)}, u32[]{:S(2)}) copy-start(bf16[1024,128]{1,0:T(8,128)(2,1)} %copy-done.19) | copy-start | bytes 786436
  363.6 8.1 %copy-start.34 = (bf16[128,3,256]{2,0,1:T(8,128)(2,1)S(1)}, bf16[128,3,256]{2,0,1:T(8,128)(2,1)}, u32[]{:S(2)}) copy-start(bf16[128,3,256]{2,0,1:T(8,128)(2,1)} %param.49) | copy-start | bytes 589828
  371.4 6.2 %copy-start.13 = (bf16[256,1024]{1,0:T(8,128)(2,1)S(1)}, bf16[256,1024]{1,0:T(8,128)(2,1)}, u32[]{:S(2)}) copy-start(bf16[256,1024]{1,0:T(8,128)(2,1)} %fusion.116) | copy-start | bytes 1572868
  371.4 8.1 %copy-start.11 = (bf16[256,1024]{1,0:T(8,128)(2,1)S(1)}, bf16[256,1024]{1,0:T(8,128)(2,1)}, u32[]{:S(2)}) copy-start(bf16[256,1024]{1,0:T(8,128)(2,1)} %convert_element_type.133) | copy-start | bytes 1572868
  371.4 78.7 %reduce-scatter.11.cloned.1.call-start = ((), (), s32[]{:S(2)}) async-start(), calls=%async_computation.11 | async-start | bytes 2949120 | tf_op jit(solution)/shard_map/reduce_scatter | solution.py:296
  377.5 3.9 copy-start.16
  377.5 6.0 copy-start.27
  377.5 6.0 copy-start.61
  377.5 215.3 %all-reduce.5.cloned.1.call-start = ((), (), s32[]{:S(2)}) async-start(), calls=%async_computation.13 | async-start | bytes 4194304 | tf_op jit(solution)/shard_map/psum | solution.py:309
  383.5 68.8 %copy-start.14 = (bf16[256,1024]{1,0:T(8,128)(2,1)S(1)}, bf16[256,1024]{1,0:T(8,128)(2,1)}, u32[]{:S(2)}) copy-start(bf16[256,1024]{1,0:T(8,128)(2,1)} %fusion.106) | copy-start | bytes 1572868
  389.1 64.3 %copy-start.3 = (bf16[256,1024]{1,0:T(8,128)(2,1)S(1)}, bf16[256,1024]{1,0:T(8,128)(2,1)}, u32[]{:S(2)}) copy-start(bf16[256,1024]{1,0:T(8,128)(2,1)} %param.31) | copy-start | bytes 1572868
  389.2 64.3 %copy-start.28 = (bf16[1024,128]{1,0:T(8,128)(2,1)S(1)}, bf16[1024,128]{1,0:T(8,128)(2,1)}, u32[]{:S(2)}) copy-start(bf16[1024,128]{1,0:T(8,128)(2,1)} %param.48) | copy-start | bytes 786436
  389.2 64.3 %copy-start.38 = (f32[256]{0:T(256)S(1)}, f32[256]{0:T(256)}, u32[]{:S(2)}) copy-start(f32[256]{0:T(256)} %copy-done.37) | copy-start | bytes 3076
  389.2 64.3 %copy-start.42 = (f32[1024]{0:T(1024)S(1)}, f32[1024]{0:T(1024)}, u32[]{:S(2)}) copy-start(f32[1024]{0:T(1024)} %param.36) | copy-start | bytes 12292
  417.5 38.4 %copy-start.46 = (f32[256]{0:T(256)S(1)}, f32[256]{0:T(256)}, u32[]{:S(2)}) copy-start(f32[256]{0:T(256)} %copy-done.45) | copy-start | bytes 3076
  418.3 38.1 %copy-start.8 = (f32[256,1024]{1,0:T(8,128)S(1)}, f32[256,1024]{1,0:T(8,128)}, u32[]{:S(2)}) copy-start(f32[256,1024]{1,0:T(8,128)} %param.32) | copy-start | bytes 3145732
  418.3 38.1 %copy-start.10 = (f32[256,1024]{1,0:T(8,128)S(1)}, f32[256,1024]{1,0:T(8,128)}, u32[]{:S(2)}) copy-start(f32[256,1024]{1,0:T(8,128)} %copy-done.9) | copy-start | bytes 3145732
  418.3 38.1 %copy-start.52 = (f32[256]{0:T(256)S(1)}, f32[256]{0:T(256)}, u32[]{:S(2)}) copy-start(f32[256]{0:T(256)} %copy-done.51) | copy-start | bytes 3076
  456.3 143.9 %copy-start.1 = (bf16[1024,128]{1,0:T(8,128)(2,1)S(1)}, bf16[1024,128]{1,0:T(8,128)(2,1)}, u32[]{:S(2)}) copy-start(bf16[1024,128]{1,0:T(8,128)(2,1)} %param.52) | copy-start | bytes 786436
  (19 other events, 35.5 us)
Sparse Core Ops, SparseCore 0:
  12.1 26.6 all-gather.6
  90.9 33.0 reduce-scatter.4
  126.2 22.5 all-gather.10
  150.9 22.5 all-gather.8
  190.9 33.0 reduce-scatter.8
  229.0 22.7 all-gather.12
  254.4 33.0 reduce-scatter.6
  292.2 73.4 all-reduce.6
  371.5 44.2 all-gather.14
  418.2 31.8 reduce-scatter.10
  457.9 134.8 all-reduce.4
